TPU v7x, 256 devices: a whole 4x4x8 slice. The times are simulated.
256 devices in a mesh: tiles: 16 (over y, z_lo, core), coef: 16 (over x, z_hi).
Axes of the slice: x: 4, y: 4, z: 8 (z_hi: 4, z_lo: 2; z = z_hi * 2 + z_lo), core: 2. Of those that a mesh axis runs over, the one named last changes fastest.
Arguments:
- fields: bfloat16 [256, 8192], P('coef', 'tiles'), may hold values from -6 to 6
- adjoints: bfloat16 [256, 8192], P('coef', 'tiles'), may hold values from -6 to 6
- couple: bfloat16 [30, 256, 256], replicated, may hold values from -0.0625 to 0.0625
- tmatrices: bfloat16 [64, 256, 256], P('tiles', 'coef'), may hold values from -0.375 to 0.375
- neighbours: int32 [8192, 30], P('tiles'), may hold values from -1 to 8191, as said below
- classes: int32 [8192], P('tiles'), may hold values from 0 to 63
Outputs:
- forward_out: bfloat16 [256, 8192], P('coef', 'tiles')
- adjoint_out: bfloat16 [256, 8192], P('coef', 'tiles')
Inputs may be any that keep to these rules, and one draw needn't show every extreme that they name: neighbours[i, m] is -1 or i + m - 15 for m < 15, or i + m - 14 for m >= 15; links are mutual: neighbours[i, m] = j >= 0 exactly when neighbours[j, 29 - m] = i; slots 15 - 1 and 15 are filled wherever the neighbouring pillar exists.
All inputs are finite; a program needn't handle non-finite values.
Results may differ from a plain program's by a relative error of at most 0.0037.
Values may be sent and summed in bfloat16 or wider, within the bound.
A program may use at most 64 MiB of HBM per device.

v0:
```python
import jax
import jax.numpy as jnp
from jax import lax
from jax.sharding import PartitionSpec as P

SLOTS = 30
HW = 15


def padded_2(cells, sides, width):
    for axis, dim in sides:
        count = lax.axis_size(axis)
        ends = count - 1
        head = lax.slice_in_dim(cells, 0, width, axis=dim)
        tail = lax.slice_in_dim(cells, cells.shape[dim] - width, cells.shape[dim], axis=dim)
        cells = jnp.concatenate(
            [
                lax.ppermute(tail, axis, [(i, (i + 1) % count) for i in range(ends)]),
                cells,
                lax.ppermute(head, axis, [((i + 1) % count, i) for i in range(ends)]),
            ],
            axis=dim,
        )
    return cells


def slot_columns(padded, weight_table, starts, width):
    pieces = [
        padded[:, start : start + width] * weight_table[slot][None, :]
        for slot, start in enumerate(starts)
    ]
    return jnp.stack(pieces, axis=1)


def local(fields, adjoints, couple, tmatrices, neighbours, classes):
    row_count = fields.shape[0]
    tile_len = fields.shape[1]
    coef_index = lax.axis_index("coef")
    is_valid = neighbours >= 0
    slot_weight = is_valid.astype(jnp.bfloat16).T
    forward_starts = [slot + (1 if slot >= HW else 0) for slot in range(SLOTS)]
    adjoint_starts = forward_starts[::-1]
    own_first = coef_index * row_count

    def translate(source, weight_table, starts, adjoint_mode):
        padded = padded_2(source, (("tiles", 1),), HW)
        own_mats = lax.dynamic_slice_in_dim(couple, own_first, row_count, 2 if adjoint_mode else 1)

        def add_piece(arrived):
            selected = slot_columns(arrived, weight_table, starts, tile_len)
            if adjoint_mode:
                block_mat = own_mats
                return jnp.einsum(
                    "nkr,kni->ri", block_mat, selected, preferred_element_type=jnp.float32
                )
            block_mat = own_mats
            return jnp.einsum(
                "nrk,kni->ri", block_mat, selected, preferred_element_type=jnp.float32
            )

        return add_piece(lax.all_gather(padded, "coef", axis=0, tiled=True))

    coupled = translate(fields, slot_weight, forward_starts, False).astype(jnp.bfloat16)
    class_rows = lax.all_gather(tmatrices, "tiles", axis=0, tiled=True)
    sub_table = class_rows
    picked = jnp.take(sub_table, classes, axis=0)
    applied = jnp.einsum(
        "irk,ki->ri",
        picked,
        lax.all_gather(coupled, "coef", axis=0, tiled=True),
        preferred_element_type=jnp.float32,
    )
    forward_out = (fields.astype(jnp.float32) - applied).astype(jnp.bfloat16)
    class_cols = lax.all_to_all(class_rows, "coef", split_axis=2, concat_axis=1, tiled=True)
    sub_table = class_cols
    picked = jnp.take(sub_table, classes, axis=0)
    scattered_sum = jnp.einsum(
        "irk,ri->ki",
        picked,
        lax.all_gather(adjoints, "coef", axis=0, tiled=True),
        preferred_element_type=jnp.float32,
    )
    scattered = scattered_sum.astype(jnp.bfloat16)
    returned = translate(scattered, slot_weight[::-1], adjoint_starts, True)
    adjoint_out = (adjoints.astype(jnp.float32) - returned).astype(jnp.bfloat16)
    return (forward_out, adjoint_out)


def solution(mesh):
    placed = (
        P("coef", "tiles"),
        P("coef", "tiles"),
        P(),
        P("tiles", "coef", None),
        P("tiles", None),
        P("tiles"),
    )
    return jax.shard_map(
        local,
        mesh=mesh,
        in_specs=placed,
        out_specs=(P("coef", "tiles"), P("coef", "tiles")),
        check_vma=False,
    )
```

profile of v0, /device:TPU:1, one launch (start us, length us, event | category | flops | bytes accessed | tf_op | source)
XLA Modules:
  0.0 256.7 jit_solution(10606946548636086392)
XLA Ops:
  0.6 0.8 fusion.138
  1.5 4.9 %collective-permute-start = (bf16[16,15]{1,0:T(8,128)(2,1)S(1)}, bf16[16,15]{1,0:T(8,128)(2,1)S(1)}, u32[]{:S(2)}, u32[]{:S(2)}) collective-permute-start(bf16[16,15]{1,0:T(8,128)(2,1)S(1)} %get-tuple-element.36), channel_id=1, source_target_pairs={{0,16},{16,32},{32,48},{48,64},{64,80},{80,96},{96,112},{112,128},... | collective-permute-start | bytes 1448 | tf_op jit(solution)/shard_map/ppermute | solution.py:18
  6.4 1.9 collective-permute-start.1
  8.3 22.9 %all_gather.17 = bf16[64,16,256]{2,1,0:T(8,128)(2,1)S(1)} all-gather(bf16[4,16,256]{2,1,0:T(8,128)(2,1)} %param.9), channel_id=1, replica_groups=mesh['tiles'=16,'coef'=16] {'tiles'}, dimensions={0}, use_global_device_ids=true | all-gather | bytes 557056 | tf_op jit(solution)/shard_map/all_gather | solution.py:64
  31.2 1.3 copy.22
  32.5 1.5 reshape.63
  34.0 9.9 %all-to-all-start = ((bf16[16,2,8192]{2,1,0:T(2,128)(2,1)}), bf16[16,2,8192]{2,1,0:T(2,128)(2,1)S(1)}, u32[]{:S(2)}, u32[]{:S(2)}) async-start(bf16[16,2,8192]{2,1,0:T(2,128)(2,1)} %reshape.63), calls=%async_computation | async-start | bytes 1048576 | tf_op jit(solution)/shard_map/all_to_all | solution.py:74
  43.9 0.8 fusion.133
  44.9 0.7 compare_select_fusion
  45.6 0.7 compare_and_fusion
  46.3 41.0 %all_gather.18 = bf16[256,512]{1,0:T(8,128)(2,1)S(1)} all-gather(bf16[16,512]{1,0:T(8,128)(2,1)} %param.7), channel_id=1, replica_groups=mesh['tiles'=16,'coef'=16] {'coef'}, dimensions={0}, use_global_device_ids=true | all-gather | bytes 278528 | tf_op jit(solution)/shard_map/all_gather | solution.py:80
  87.3 3.4 %gather_fusion = bf16[512,16,256]{2,1,0:T(8,128)(2,1)} fusion(bf16[64,16,256]{2,1,0:T(8,128)(2,1)S(1)} %all_gather.17, s32[1024]{0:T(1024)S(1)} %pad_clamp_fusion), kind=kCustom, calls=%fused_computation | custom fusion | bytes 8390656 | tf_op jit(solution)/shard_map/jit(_take)/gather | solution.py:66
  90.8 0.2 copy.40
  91.1 36.5 %all_gather.15 = bf16[256,542]{1,0:T(8,128)(2,1)S(1)} all-gather(bf16[16,542]{1,0:T(8,128)(2,1)S(1)} %pad_maximum_fusion), channel_id=1, replica_groups=mesh['tiles'=16,'coef'=16] {'coef'}, dimensions={0}, use_global_device_ids=true | all-gather | bytes 294848 | tf_op jit(solution)/shard_map/all_gather | solution.py:61
  127.6 0.1 fusion.129
  127.8 0.1 fusion.127
  128.1 0.1 fusion.123
  128.4 0.1 fusion.119
  128.5 0.1 fusion.117
  128.7 0.1 fusion.115
  128.8 0.1 fusion.113
  129.1 0.1 fusion.109
  129.4 0.1 fusion.105
  129.5 0.1 fusion.103
  129.7 0.1 fusion.101
  129.8 0.1 fusion.99
  130.1 0.1 fusion.95
  130.4 0.1 fusion.91
  130.6 0.1 fusion.89
  130.9 0.1 fusion.85
  131.2 0.1 fusion.81
  131.3 0.1 fusion.79
  131.5 0.1 fusion.77
  131.6 0.1 fusion.75
  131.9 2.1 fusion.8
  134.0 32.7 %all_gather.16 = bf16[256,512]{1,0:T(8,128)(2,1)S(1)} all-gather(bf16[16,512]{1,0:T(8,128)(2,1)S(1)} %fusion.8), channel_id=1, replica_groups=mesh['tiles'=16,'coef'=16] {'coef'}, dimensions={0}, use_global_device_ids=true | all-gather | bytes 278528 | tf_op jit(solution)/shard_map/all_gather | solution.py:70
  166.7 0.2 copy.39
  166.9 0.7 reshape.64
  167.6 0.3 copy.24
  167.9 1.3 copy.25
  169.2 3.5 %gather_fusion.1 = bf16[512,256,16]{1,2,0:T(8,128)(2,1)} fusion(bf16[64,256,16]{1,2,0:T(8,128)(2,1)S(1)} %copy.25, s32[1024]{0:T(1024)S(1)} %pad_clamp_fusion), kind=kCustom, calls=%fused_computation.1 | custom fusion | bytes 8390656 | tf_op jit(solution)/shard_map/jit(_take)/gather | solution.py:76
  172.7 13.6 %multiply_reduce_fusion = (bf16[512,16]{1,0:T(8,128)(2,1)S(1)}, f32[512,16]{1,0:T(8,128)S(1)}) fusion(f32[512,256]{1,0:T(8,128)S(1)} %copy.40, bf16[512,256,16]{1,2,0:T(8,128)(2,1)} %gather_fusion.1, pred[512]{0:T(512)(128)(4,1)S(1)} %compare_and_fusion, bf16[512,16,256]{2,1,0:T(8,128)(2,1)} %gather_fusion, f32[512,256]{1,0:T(8,128)S(1)} %copy.39), kind=kLoop, calls=%fused_computation.2 | loop fusion | flops 16760832 | bytes 9486848
  186.5 23.8 %collective-permute-start.2 = (bf16[16,15]{1,0:T(8,128)(2,1)S(1)}, bf16[16,15]{1,0:T(8,128)(2,1)S(1)}, u32[]{:S(2)}, u32[]{:S(2)}) collective-permute-start(bf16[16,15]{1,0:T(8,128)(2,1)S(1)} %get-tuple-element.34), channel_id=1, source_target_pairs={{0,16},{16,32},{32,48},{48,64},{64,80},{80,96},{96,112},{112,128},... | collective-permute-start | bytes 1448 | tf_op jit(solution)/shard_map/ppermute | solution.py:18
  210.3 1.9 collective-permute-start.3
  212.3 0.6 fusion.134
  213.0 2.3 collective-permute-done.3
  215.3 34.8 %all_gather.19 = bf16[256,542]{1,0:T(8,128)(2,1)S(1)} all-gather(bf16[16,542]{1,0:T(8,128)(2,1)S(1)} %pad_maximum_fusion.1), channel_id=1, replica_groups=mesh['tiles'=16,'coef'=16] {'coef'}, dimensions={0}, use_global_device_ids=true | all-gather | bytes 294848 | tf_op jit(solution)/shard_map/all_gather | solution.py:61
  250.3 0.1 fusion.69
  250.6 0.1 fusion.65
  250.9 0.1 fusion.61
  251.0 0.1 fusion.59
  251.2 0.1 fusion.57
  251.3 0.1 fusion.55
  251.6 0.1 fusion.51
  251.9 0.1 fusion.47
  252.0 0.1 fusion.45
  252.2 0.1 fusion.43
  252.3 0.1 fusion.41
  252.6 0.1 fusion.37
  252.9 0.1 fusion.33
  253.1 0.1 fusion.31
  253.4 0.1 fusion.27
  253.7 0.1 fusion.23
  254.5 2.2 fusion.9
  (44 shorter events, 3.9 us)
Async XLA Ops:
  0.6 90.4 %copy-start.1 = (bf16[16,512]{1,0:T(8,128)(2,1)S(1)}, bf16[16,512]{1,0:T(8,128)(2,1)}, u32[]{:S(2)}) copy-start(bf16[16,512]{1,0:T(8,128)(2,1)} %param.6) | copy-start | bytes 49156
  1.5 89.5 %collective-permute-start = (bf16[16,15]{1,0:T(8,128)(2,1)S(1)}, bf16[16,15]{1,0:T(8,128)(2,1)S(1)}, u32[]{:S(2)}, u32[]{:S(2)}) collective-permute-start(bf16[16,15]{1,0:T(8,128)(2,1)S(1)} %get-tuple-element.36), channel_id=1, source_target_pairs={{0,16},{16,32},{32,48},{48,64},{64,80},{80,96},{96,112},{112,128},... | collective-permute-start | bytes 1448 | tf_op jit(solution)/shard_map/ppermute | solution.py:18
  6.4 84.6 %collective-permute-start.1 = (bf16[16,15]{1,0:T(8,128)(2,1)S(1)}, bf16[16,15]{1,0:T(8,128)(2,1)S(1)}, u32[]{:S(2)}, u32[]{:S(2)}) collective-permute-start(bf16[16,15]{1,0:T(8,128)(2,1)S(1)} %get-tuple-element.37), channel_id=1, source_target_pairs={{16,0},{32,16},{48,32},{64,48},{80,64},{96,80},{112,96},{128,112},... | collective-permute-start | bytes 1448 | tf_op jit(solution)/shard_map/ppermute | solution.py:20
  34.0 132.9 %all-to-all-start = ((bf16[16,2,8192]{2,1,0:T(2,128)(2,1)}), bf16[16,2,8192]{2,1,0:T(2,128)(2,1)S(1)}, u32[]{:S(2)}, u32[]{:S(2)}) async-start(bf16[16,2,8192]{2,1,0:T(2,128)(2,1)} %reshape.63), calls=%async_computation | async-start | bytes 1048576 | tf_op jit(solution)/shard_map/all_to_all | solution.py:74
  186.5 26.5 %collective-permute-start.2 = (bf16[16,15]{1,0:T(8,128)(2,1)S(1)}, bf16[16,15]{1,0:T(8,128)(2,1)S(1)}, u32[]{:S(2)}, u32[]{:S(2)}) collective-permute-start(bf16[16,15]{1,0:T(8,128)(2,1)S(1)} %get-tuple-element.34), channel_id=1, source_target_pairs={{0,16},{16,32},{32,48},{48,64},{64,80},{80,96},{96,112},{112,128},... | collective-permute-start | bytes 1448 | tf_op jit(solution)/shard_map/ppermute | solution.py:18
  210.3 4.9 %collective-permute-start.3 = (bf16[16,15]{1,0:T(8,128)(2,1)S(1)}, bf16[16,15]{1,0:T(8,128)(2,1)S(1)}, u32[]{:S(2)}, u32[]{:S(2)}) collective-permute-start(bf16[16,15]{1,0:T(8,128)(2,1)S(1)} %get-tuple-element.35), channel_id=1, source_target_pairs={{16,0},{32,16},{48,32},{64,48},{80,64},{96,80},{112,96},{128,112},... | collective-permute-start | bytes 1448 | tf_op jit(solution)/shard_map/ppermute | solution.py:20
  250.1 4.3 %copy-start = (bf16[30,256,256]{2,1,0:T(8,128)(2,1)S(1)}, bf16[30,256,256]{2,1,0:T(8,128)(2,1)}, u32[]{:S(2)}) copy-start(bf16[30,256,256]{2,1,0:T(8,128)(2,1)} %param.8) | copy-start | bytes 11796484
  250.1 4.3 %copy-start.2 = (bf16[16,512]{1,0:T(8,128)(2,1)S(1)}, bf16[16,512]{1,0:T(8,128)(2,1)}, u32[]{:S(2)}) copy-start(bf16[16,512]{1,0:T(8,128)(2,1)} %param.7) | copy-start | bytes 49156
where the time goes:
time: 261 us; the launch traced here: 257 us
  blocking collectives  168 us (64%)
  starting transfers between devices  42.5 us (16%)
  other arithmetic  24.9 us (10%)
  local copies, waits for them, and re-layouts  13.7 us (5%)
  matrix products  4.25 us (2%)
    all_gather x2, blocking collectives, translate(): return add_piece(lax.all_gather(padded, 'coef', axis=0, tiled=True))  71.3 us
    all_gather x1, blocking collectives, local(): lax.all_gather(adjoints, 'coef', axis=0, tiled=True)  41 us
    all_gather x1, blocking collectives, local(): lax.all_gather(coupled, 'coef', axis=0, tiled=True)  32.7 us
    ppermute x2, starting transfers between devices, padded_2(): lax.ppermute(tail, axis, [(i, (i + 1) % count) for i in range(ends)])  28.8 us
    all_gather x1, blocking collectives, local(): class_rows = lax.all_gather(tmatrices, 'tiles', axis=0, tiled=True)  22.9 us
    unnamed x61, other arithmetic  21.7 us
    all_to_all x1, starting transfers between devices, local(): lax.all_to_all(class_rows, 'coef', split_axis=2, concat_axis=1, tiled=True)  9.85 us
    gather x2, local copies, waits for them, and re-layouts, local(): picked = jnp.take(sub_table, classes, axis=0)  6.91 us
  transfers between devices with their start and end apart: 5, of which 1 were waited for; matrix products, arithmetic and copies ran while one was open for 6% of the time, Pallas kernels for 0%

commit v1 on v0

v1 whole, which is shorter than its diff:
```python
import functools

import jax
import jax.numpy as jnp
from jax import lax
from jax.experimental import pallas as pl
from jax.experimental.pallas import tpu as pltpu
from jax.sharding import PartitionSpec as P

SLOTS = 30
HW = 15
LANE = 128
MESH = pl.DeviceIdType.MESH
F32 = jnp.float32
BF16 = jnp.bfloat16


def dims(lhs, rhs):
    return (((lhs,), (rhs,)), ((), ()))


def dot(a, b, lhs=1, rhs=0):
    return lax.dot_general(a, b, dims(lhs, rhs), preferred_element_type=F32)


def kernel(
    fields_h, adj_h, couple_h, tmat_h, nbr_h, cls_h, fwd_ref, adjo_ref,
    fields, adj, nbr, cls, rows_w, slab, cols_w, mask, t_all,
    edge_f, edge_a, edge_c, fh_all, ah, clsh, expanded, part, landed, coup_all, s_all,
    load_sem, t_send, t_recv, tc_send, tc_recv, e_send, e_recv,
    f_send, f_recv, p_send, p_recv, c_send, c_recv, s_send, s_recv,
):
    rows, width = fields.shape
    wide = ah.shape[1]
    t, c = lax.axis_index("tiles"), lax.axis_index("coef")
    n_t, n_c = 16, 16
    mate = t + 1 - 2 * lax.rem(t, 2)

    def tile_at(step):
        return lax.rem(t + step, n_t)

    def coef_at(step):
        return lax.rem(c + step, n_c)

    own = pl.ds(pl.multiple_of(c * rows, rows), rows)
    lane0 = pl.multiple_of((c // 8) * LANE, LANE)

    loads = [
        pltpu.make_async_copy(fields_h, fields, load_sem.at[0]),
        pltpu.make_async_copy(adj_h, adj, load_sem.at[1]),
        pltpu.make_async_copy(tmat_h, t_all.at[pl.ds(t * 4, 4)], load_sem.at[2]),
        pltpu.make_async_copy(cls_h, cls, load_sem.at[3]),
        pltpu.make_async_copy(nbr_h, nbr, load_sem.at[4]),
        pltpu.make_async_copy(couple_h.at[:, :, pl.ds(lane0, LANE)], slab, load_sem.at[5]),
        pltpu.make_async_copy(couple_h.at[:, own, :], rows_w, load_sem.at[6]),
    ]
    for load in loads:
        load.start()

    barrier = pltpu.get_barrier_semaphore()
    for step in (1, 15, 2, 4, 6, 8, 10, 12, 14):
        pl.semaphore_signal(barrier, inc=1, device_id=(tile_at(step), c), device_id_type=MESH)
    for step in range(1, n_c):
        pl.semaphore_signal(barrier, inc=1, device_id=(t, coef_at(step)), device_id_type=MESH)
    for load in loads[:4]:
        load.wait()
    pl.semaphore_wait(barrier, 9 + n_c - 1)

    def remote(src, dst, send, recv, tile, coef):
        return pltpu.make_async_remote_copy(
            src_ref=src, dst_ref=dst, send_sem=send, recv_sem=recv,
            device_id=(tile, coef), device_id_type=MESH,
        )

    def shard(tile):
        return t_all.at[pl.ds(tile * 4, 4)]

    t_copies = [
        remote(shard(t), shard(t), t_send.at[s], t_recv.at[s], tile_at(2 * s), c) for s in range(1, 8)
    ]
    mate_copies = [remote(shard(t), shard(t), tc_send.at[0], tc_recv.at[0], mate, c)]
    for s in (4, 3, 5, 2, 6, 1, 7):
        t_copies[s - 1].start()
    first, last = pl.ds(0, LANE), pl.ds(width - LANE, LANE)
    edges = []
    for k, (src, dst) in enumerate(((adj, edge_a), (cls, edge_c), (fields, edge_f))):
        edges.append(remote(src.at[:, first], dst.at[0], e_send.at[2 * k], e_recv.at[2 * k], tile_at(15), c))
        edges.append(remote(src.at[:, last], dst.at[1], e_send.at[2 * k + 1], e_recv.at[2 * k + 1], tile_at(1), c))
    for edge in edges:
        edge.start()
    mate_copies[0].start()

    loads[4].wait()
    eye = (
        lax.broadcasted_iota(jnp.int32, (32, SLOTS), 0) == lax.broadcasted_iota(jnp.int32, (32, SLOTS), 1)
    ).astype(F32).astype(BF16)
    linked = (nbr[...] >= 0).astype(F32).astype(BF16)
    mask[...] = dot(eye, linked, 1, 1)

    ah[:, :width] = adj[...]
    clsh[:, :width] = cls[...]
    fh_all[own, :width] = fields[...]
    for edge in edges:
        edge.wait_recv()
    low = lax.broadcasted_iota(jnp.int32, (rows, LANE), 1) < LANE // 2
    low_row = lax.broadcasted_iota(jnp.int32, (1, LANE), 1) < LANE // 2
    ah[:, width:] = jnp.where(low, edge_a[0], edge_a[1])
    clsh[:, width:] = jnp.where(low_row, edge_c[0], edge_c[1])
    fh_all[own, width:] = jnp.where(low, edge_f[0], edge_f[1])

    order = (10, 6, 9, 11, 5, 7, 2, 14, 8, 13, 3, 1, 15, 4, 12)
    f_copies = {
        s: remote(fh_all.at[own], fh_all.at[own], f_send.at[s], f_recv.at[s], t, coef_at(s)) for s in order
    }
    for s in order:
        f_copies[s].start()

    adj_f = ah[...].astype(F32)
    cls_rows = jnp.broadcast_to(clsh[...], (rows, wide))
    for k in range(64):
        expanded[k * rows : (k + 1) * rows, :] = jnp.where(cls_rows == k, adj_f, 0.0).astype(BF16)

    loads[5].wait()
    loads[6].wait()
    pick = (
        lax.broadcasted_iota(jnp.int32, (rows, LANE), 1)
        == lax.broadcasted_iota(jnp.int32, (rows, LANE), 0) + lax.rem(c, 8) * rows
    ).astype(F32).astype(BF16)
    for m in range(SLOTS):
        cols_w[m] = dot(pick, slab[SLOTS - 1 - m], 1, 1).astype(BF16)

    for s in (1, 7, 2, 6, 3, 5, 4):
        t_copies[s - 1].wait_recv()
        came = tile_at(16 - 2 * s)
        passed = remote(shard(came), shard(came), tc_send.at[s], tc_recv.at[s], mate, c)
        passed.start()
        mate_copies.append(passed)
    for copy in mate_copies:
        copy.wait_recv()

    t_rows = t_all[...].reshape(64 * rows, 256)
    part[...] = dot(t_rows, expanded[...], 0, 0).astype(BF16)
    p_copies = {}
    for s in order:
        block = pl.ds(pl.multiple_of(coef_at(s) * rows, rows), rows)
        p_copies[s] = remote(part.at[block], landed.at[s], p_send.at[s], p_recv.at[s], t, coef_at(s))
        p_copies[s].start()

    def coupling(weights, source):
        product = dot(weights, source)
        total = jnp.zeros((rows, width), F32)
        for m in range(SLOTS):
            shift = m - HW + (1 if m >= HW else 0)
            rolled = pltpu.roll(product[m * rows : (m + 1) * rows], (-shift) % wide, 1)
            total += rolled[:, :width] * mask[m : m + 1, :]
        return total

    for s in order:
        f_copies[s].wait_recv()
    coup_all[own, :] = coupling(rows_w[...].reshape(SLOTS * rows, 256), fh_all[...]).astype(BF16)
    c_copies = {
        s: remote(coup_all.at[own], coup_all.at[own], c_send.at[s], c_recv.at[s], t, coef_at(s)) for s in order
    }
    for s in order:
        c_copies[s].start()

    total = part[own, :].astype(F32)
    for s in order:
        p_copies[s].wait_recv()
        total += landed[s].astype(F32)
    s_all[own, :] = total.astype(BF16)
    s_copies = {
        s: remote(s_all.at[own], s_all.at[own], s_send.at[s], s_recv.at[s], t, coef_at(s)) for s in order
    }
    for s in order:
        s_copies[s].start()

    for s in order:
        c_copies[s].wait_recv()
    cls_own = jnp.broadcast_to(cls[...], (rows, width))
    applied = jnp.zeros((rows, width), F32)
    for b in range(4):
        product = dot(t_all[16 * b : 16 * b + 16].reshape(16 * rows, 256), coup_all[...])
        for k in range(16):
            applied += jnp.where(cls_own == 16 * b + k, product[k * rows : (k + 1) * rows], 0.0)
    fwd_ref[...] = (fields[...].astype(F32) - applied).astype(BF16)

    for s in order:
        s_copies[s].wait_recv()
    returned = coupling(cols_w[...].reshape(SLOTS * rows, 256), s_all[...])
    adjo_ref[...] = (adj[...].astype(F32) - returned).astype(BF16)

    for copy in t_copies + mate_copies + edges:
        copy.wait_send()
    for group in (f_copies, p_copies, c_copies, s_copies):
        for s in order:
            group[s].wait_send()


def local(fields, adjoints, couple, tmatrices, neighbours, classes):
    rows, width = fields.shape
    wide = width + LANE
    kr = couple.shape[1]
    dma = pltpu.SemaphoreType.DMA
    anywhere = pl.BlockSpec(memory_space=pl.ANY)
    vmem = pl.BlockSpec(memory_space=pltpu.VMEM)
    return pl.pallas_call(
        kernel,
        out_shape=(jax.ShapeDtypeStruct((rows, width), BF16),) * 2,
        in_specs=[anywhere] * 6,
        out_specs=(vmem, vmem),
        scratch_shapes=[
            pltpu.VMEM((rows, width), BF16),
            pltpu.VMEM((rows, width), BF16),
            pltpu.VMEM((width, SLOTS), jnp.int32),
            pltpu.VMEM((1, width), jnp.int32),
            pltpu.VMEM((SLOTS, rows, kr), BF16),
            pltpu.VMEM((SLOTS, kr, LANE), BF16),
            pltpu.VMEM((SLOTS, rows, kr), BF16),
            pltpu.VMEM((32, width), F32),
            pltpu.VMEM((64, rows, kr), BF16),
            pltpu.VMEM((2, rows, LANE), BF16),
            pltpu.VMEM((2, rows, LANE), BF16),
            pltpu.VMEM((2, 1, LANE), jnp.int32),
            pltpu.VMEM((kr, wide), BF16),
            pltpu.VMEM((rows, wide), BF16),
            pltpu.VMEM((1, wide), jnp.int32),
            pltpu.VMEM((64 * rows, wide), BF16),
            pltpu.VMEM((kr, wide), BF16),
            pltpu.VMEM((16, rows, wide), BF16),
            pltpu.VMEM((kr, width), BF16),
            pltpu.VMEM((kr, wide), BF16),
            dma((7,)), dma((8,)), dma((8,)), dma((8,)), dma((8,)), dma((6,)), dma((6,)),
            dma((16,)), dma((16,)), dma((16,)), dma((16,)), dma((16,)), dma((16,)), dma((16,)), dma((16,)),
        ],
        compiler_params=pltpu.CompilerParams(
            collective_id=0, has_side_effects=True, vmem_limit_bytes=48 * 1024 * 1024
        ),
    )(fields, adjoints, couple, tmatrices, neighbours, classes.reshape(1, width))


def solution(mesh):
    placed = (
        P("coef", "tiles"),
        P("coef", "tiles"),
        P(),
        P("tiles", "coef", None),
        P("tiles", None),
        P("tiles"),
    )
    return jax.shard_map(
        local,
        mesh=mesh,
        in_specs=placed,
        out_specs=(P("coef", "tiles"), P("coef", "tiles")),
        check_vma=False,
    )
```

time: 261 us -> 64.1 us (0.25); the launches traced: 257 us -> 63.7 us
  blocking collectives: 168 us -> 0 us
  Pallas kernels: 0 us -> 55.9 us
  starting transfers between devices: 42.5 us -> 0 us
  other arithmetic: 24.9 us -> 0 us
  local copies, waits for them, and re-layouts: 13.7 us -> 7.17 us
  matrix products: 4.25 us -> 0 us
    all_gather x5 -> x0, blocking collectives: 168 us -> none  [the longest x2 71.3 us: translate(): return add_piece(lax.all_gather(padded, 'coef', axis=0, tiled=True))]
    pallas_call x0 -> x1, Pallas kernels: none -> 55.9 us  [local(): pl.pallas_call(kernel, out_shape=(jax.ShapeDtypeStruct((rows, width), BF1...]
    ppermute x4 -> x0, starting transfers between devices: 32.6 us -> none  [the longest x2 28.8 us: padded_2(): lax.ppermute(tail, axis, [(i, (i + 1) % count) for i in range(ends)])]
    unnamed x61 -> x0, other arithmetic: 21.7 us -> none
    all_to_all x1 -> x0, starting transfers between devices: 9.85 us -> none  [local(): lax.all_to_all(class_rows, 'coef', split_axis=2, concat_axis=1, tiled=True)]
    gather x2 -> x0, local copies, waits for them, and re-layouts: 6.91 us -> none  [local(): picked = jnp.take(sub_table, classes, axis=0)]
    unnamed x10 -> x13, local copies, waits for them, and re-layouts: 2.57 us -> 7.17 us
    dot_general x2 -> x0, matrix products: 4.25 us -> none  [the longest x1 2.18 us: add_piece(): jnp.einsum('nkr,kni->ri', block_mat, selected, preferred_element_type=jnp...]
  transfers between devices with their start and end apart: 5 -> 0, of which waited for: 1 -> 0; matrix products, arithmetic and copies ran while one was open for 6% -> 0% of each run, Pallas kernels for 0% -> 0%
where the time goes in v1:
time: 64.1 us; the launch traced here: 63.7 us
  Pallas kernels  55.9 us (87%)
  local copies, waits for them, and re-layouts  7.17 us (11%)
  between operations  0.66 us (1%)
    pallas_call x1, Pallas kernels, local(): pl.pallas_call(kernel, out_shape=(jax.ShapeDtypeStruct((rows, width), BF1...  55.9 us
    unnamed x13, local copies, waits for them, and re-layouts  7.17 us

profile of v1, /device:TPU:1, one launch (start us, length us, event | category | flops | bytes accessed | tf_op | source)
XLA Modules:
  0.0 63.7 jit_solution(10303887447909387237)
XLA Ops:
  0.6 1.0 %copy.8.nbr_h = s32[512,30]{1,0:T(8,128)S(1)} copy(s32[512,30]{0,1:T(8,128)} %param.10) | data formatting | bytes 122880 | tf_op args[4]
  1.6 0.0 copy-start
  1.6 2.1 %copy-done = bf16[30,256,256]{2,1,0:T(8,128)(2,1)S(1)} copy-done((bf16[30,256,256]{2,1,0:T(8,128)(2,1)S(1)}, bf16[30,256,256]{2,1,0:T(8,128)(2,1)}, u32[]{:S(2)}) %copy-start) | copy-done | bytes 3932184
  3.7 0.0 copy-start.1
  3.7 0.8 %copy-done.1 = bf16[4,16,256]{2,1,0:T(8,128)(2,1)S(1)} copy-done((bf16[4,16,256]{2,1,0:T(8,128)(2,1)S(1)}, bf16[4,16,256]{2,1,0:T(8,128)(2,1)}, u32[]{:S(2)}) %copy-start.1) | copy-done | bytes 32792
  4.5 0.0 copy-start.2
  4.5 0.7 %copy-done.2 = bf16[16,512]{1,0:T(8,128)(2,1)S(1)} copy-done((bf16[16,512]{1,0:T(8,128)(2,1)S(1)}, bf16[16,512]{1,0:T(8,128)(2,1)}, u32[]{:S(2)}) %copy-start.2) | copy-done | bytes 16408
  5.2 0.0 copy-start.3
  5.2 0.7 %copy-done.3 = bf16[16,512]{1,0:T(8,128)(2,1)S(1)} copy-done((bf16[16,512]{1,0:T(8,128)(2,1)S(1)}, bf16[16,512]{1,0:T(8,128)(2,1)}, u32[]{:S(2)}) %copy-start.3) | copy-done | bytes 16408
  5.9 0.0 copy-start.4
  5.9 0.7 %copy-done.4 = s32[512]{0:T(512)S(1)} copy-done((s32[512]{0:T(512)S(1)}, s32[512]{0:T(512)}, u32[]{:S(2)}) %copy-start.4) | copy-done | bytes 2072
  6.6 55.9 %shard_map.77 = (bf16[16,512]{1,0:T(8,128)(2,1)S(1)}, bf16[16,512]{1,0:T(8,128)(2,1)S(1)}) custom-call(bf16[16,512]{1,0:T(8,128)(2,1)S(1)} %copy-done.2, bf16[16,512]{1,0:T(8,128)(2,1)S(1)} %copy-done.3, bf16[30,256,256]{2,1,0:T(8,128)(2,1)S(1)} %copy-done, bf16[4,16,256]{2,1,0:T(8,128)(2,1)S(1)} %copy-done.1, s32[512,30]{1,0:T(8,128)S(1)} %copy.8.nbr_h, ...), custom_call_target="tpu_custom_call" | custom-call | tf_op jit(solution)/shard_map/pallas_call | solution.py:207
  62.5 0.6 copy.11
  63.1 0.6 copy.12
Async XLA Ops:
  1.6 2.1 %copy-start = (bf16[30,256,256]{2,1,0:T(8,128)(2,1)S(1)}, bf16[30,256,256]{2,1,0:T(8,128)(2,1)}, u32[]{:S(2)}) copy-start(bf16[30,256,256]{2,1,0:T(8,128)(2,1)} %couple_h.1) | copy-start | bytes 11796484
  3.7 0.8 %copy-start.1 = (bf16[4,16,256]{2,1,0:T(8,128)(2,1)S(1)}, bf16[4,16,256]{2,1,0:T(8,128)(2,1)}, u32[]{:S(2)}) copy-start(bf16[4,16,256]{2,1,0:T(8,128)(2,1)} %tmat_h.1) | copy-start | bytes 98308
  4.5 0.7 %copy-start.2 = (bf16[16,512]{1,0:T(8,128)(2,1)S(1)}, bf16[16,512]{1,0:T(8,128)(2,1)}, u32[]{:S(2)}) copy-start(bf16[16,512]{1,0:T(8,128)(2,1)} %fields_h.1) | copy-start | bytes 49156
  5.2 0.7 %copy-start.3 = (bf16[16,512]{1,0:T(8,128)(2,1)S(1)}, bf16[16,512]{1,0:T(8,128)(2,1)}, u32[]{:S(2)}) copy-start(bf16[16,512]{1,0:T(8,128)(2,1)} %adj_h.1) | copy-start | bytes 49156
  5.9 0.7 %copy-start.4 = (s32[512]{0:T(512)S(1)}, s32[512]{0:T(512)}, u32[]{:S(2)}) copy-start(s32[512]{0:T(512)} %param.11) | copy-start | bytes 6148

commit v2 on v1

--- a/solution.py
+++ b/solution.py
@@ -42,6 +42,9 @@
     def coef_at(step):
         return lax.rem(c + step, n_c)
 
+    def peer(dx, dz):
+        return lax.rem(c // 4 + dx, 4) * 4 + lax.rem(lax.rem(c, 4) + dz, 4)
+
     own = pl.ds(pl.multiple_of(c * rows, rows), rows)
     lane0 = pl.multiple_of((c // 8) * LANE, LANE)
 
@@ -74,6 +77,41 @@
 
     def shard(tile):
         return t_all.at[pl.ds(tile * 4, 4)]
+
+    class Gather:
+        def __init__(self, buf, send, recv):
+            self.copies = {}
+            self.buf, self.send, self.recv = buf, send, recv
+
+        def start(self, source, dx, dz, slot):
+            block = self.buf.at[pl.ds(pl.multiple_of(source * rows, rows), rows)]
+            copy = remote(block, block, self.send.at[slot], self.recv.at[slot], t, peer(dx, dz))
+            copy.start()
+            self.copies[slot] = copy
+
+        def begin(self):
+            for dz in (2, 1, 3):
+                self.start(c, 0, dz, dz)
+            for dx in (2, 1, 3):
+                self.start(c, dx, 0, 4 * dx)
+
+        def relay(self, dz):
+            self.copies[dz].wait_recv()
+            for dx in (2, 1, 3):
+                self.start(peer(0, 4 - dz), dx, 0, 4 * dx + dz)
+
+        def finish(self):
+            for dz in (0, 1, 3, 2):
+                for dx in (1, 3, 2):
+                    self.copies[4 * dx + dz].wait_recv()
+
+        def drain(self):
+            for copy in self.copies.values():
+                copy.wait_send()
+
+    gather_f = Gather(fh_all, f_send, f_recv)
+    gather_c = Gather(coup_all, c_send, c_recv)
+    gather_s = Gather(s_all, s_send, s_recv)
 
     t_copies = [
         remote(shard(t), shard(t), t_send.at[s], t_recv.at[s], tile_at(2 * s), c) for s in range(1, 8)
@@ -91,11 +129,7 @@
     mate_copies[0].start()
 
     loads[4].wait()
-    eye = (
-        lax.broadcasted_iota(jnp.int32, (32, SLOTS), 0) == lax.broadcasted_iota(jnp.int32, (32, SLOTS), 1)
-    ).astype(F32).astype(BF16)
-    linked = (nbr[...] >= 0).astype(F32).astype(BF16)
-    mask[...] = dot(eye, linked, 1, 1)
+    mask[...] = (nbr[...] >= 0).astype(F32)
 
     ah[:, :width] = adj[...]
     clsh[:, :width] = cls[...]
@@ -108,12 +142,7 @@
     clsh[:, width:] = jnp.where(low_row, edge_c[0], edge_c[1])
     fh_all[own, width:] = jnp.where(low, edge_f[0], edge_f[1])
 
-    order = (10, 6, 9, 11, 5, 7, 2, 14, 8, 13, 3, 1, 15, 4, 12)
-    f_copies = {
-        s: remote(fh_all.at[own], fh_all.at[own], f_send.at[s], f_recv.at[s], t, coef_at(s)) for s in order
-    }
-    for s in order:
-        f_copies[s].start()
+    gather_f.begin()
 
     adj_f = ah[...].astype(F32)
     cls_rows = jnp.broadcast_to(clsh[...], (rows, wide))
@@ -140,11 +169,14 @@
 
     t_rows = t_all[...].reshape(64 * rows, 256)
     part[...] = dot(t_rows, expanded[...], 0, 0).astype(BF16)
-    p_copies = {}
-    for s in order:
-        block = pl.ds(pl.multiple_of(coef_at(s) * rows, rows), rows)
-        p_copies[s] = remote(part.at[block], landed.at[s], p_send.at[s], p_recv.at[s], t, coef_at(s))
-        p_copies[s].start()
+    p_copies = []
+    for dx, dz in ((2, 2), (2, 1), (2, 3), (1, 2), (3, 2), (0, 2), (1, 1), (3, 1), (1, 3), (3, 3), (0, 1), (0, 3), (2, 0), (1, 0), (3, 0)):
+        to, slot = peer(dx, dz), 4 * dx + dz
+        block = pl.ds(pl.multiple_of(to * rows, rows), rows)
+        p_copies.append(remote(part.at[block], landed.at[slot], p_send.at[slot], p_recv.at[slot], t, to))
+        p_copies[-1].start()
+    for dz in (1, 3, 2):
+        gather_f.relay(dz)
 
     def coupling(weights, source):
         product = dot(weights, source)
@@ -155,28 +187,23 @@
             total += rolled[:, :width] * mask[m : m + 1, :]
         return total
 
-    for s in order:
-        f_copies[s].wait_recv()
+    gather_f.finish()
     coup_all[own, :] = coupling(rows_w[...].reshape(SLOTS * rows, 256), fh_all[...]).astype(BF16)
-    c_copies = {
-        s: remote(coup_all.at[own], coup_all.at[own], c_send.at[s], c_recv.at[s], t, coef_at(s)) for s in order
-    }
-    for s in order:
-        c_copies[s].start()
+    gather_c.begin()
 
     total = part[own, :].astype(F32)
-    for s in order:
-        p_copies[s].wait_recv()
-        total += landed[s].astype(F32)
+    for copy in p_copies[::-1]:
+        copy.wait_recv()
+    for slot in range(1, 16):
+        total += landed[slot].astype(F32)
     s_all[own, :] = total.astype(BF16)
-    s_copies = {
-        s: remote(s_all.at[own], s_all.at[own], s_send.at[s], s_recv.at[s], t, coef_at(s)) for s in order
-    }
-    for s in order:
-        s_copies[s].start()
-
-    for s in order:
-        c_copies[s].wait_recv()
+    gather_s.begin()
+    for dz in (1, 3, 2):
+        gather_c.relay(dz)
+    for dz in (1, 3, 2):
+        gather_s.relay(dz)
+
+    gather_c.finish()
     cls_own = jnp.broadcast_to(cls[...], (rows, width))
     applied = jnp.zeros((rows, width), F32)
     for b in range(4):
@@ -185,16 +212,14 @@
             applied += jnp.where(cls_own == 16 * b + k, product[k * rows : (k + 1) * rows], 0.0)
     fwd_ref[...] = (fields[...].astype(F32) - applied).astype(BF16)
 
-    for s in order:
-        s_copies[s].wait_recv()
+    gather_s.finish()
     returned = coupling(cols_w[...].reshape(SLOTS * rows, 256), s_all[...])
     adjo_ref[...] = (adj[...].astype(F32) - returned).astype(BF16)
 
-    for copy in t_copies + mate_copies + edges:
+    for copy in t_copies + mate_copies + edges + p_copies:
         copy.wait_send()
-    for group in (f_copies, p_copies, c_copies, s_copies):
-        for s in order:
-            group[s].wait_send()
+    for gather in (gather_f, gather_c, gather_s):
+        gather.drain()
 
 
 def local(fields, adjoints, couple, tmatrices, neighbours, classes):
@@ -212,12 +237,12 @@
         scratch_shapes=[
             pltpu.VMEM((rows, width), BF16),
             pltpu.VMEM((rows, width), BF16),
-            pltpu.VMEM((width, SLOTS), jnp.int32),
+            pltpu.VMEM((SLOTS, width), jnp.int32),
             pltpu.VMEM((1, width), jnp.int32),
             pltpu.VMEM((SLOTS, rows, kr), BF16),
             pltpu.VMEM((SLOTS, kr, LANE), BF16),
             pltpu.VMEM((SLOTS, rows, kr), BF16),
-            pltpu.VMEM((32, width), F32),
+            pltpu.VMEM((SLOTS, width), F32),
             pltpu.VMEM((64, rows, kr), BF16),
             pltpu.VMEM((2, rows, LANE), BF16),
             pltpu.VMEM((2, rows, LANE), BF16),
@@ -234,9 +259,9 @@
             dma((16,)), dma((16,)), dma((16,)), dma((16,)), dma((16,)), dma((16,)), dma((16,)), dma((16,)),
         ],
         compiler_params=pltpu.CompilerParams(
-            collective_id=0, has_side_effects=True, vmem_limit_bytes=48 * 1024 * 1024
+            collective_id=0, has_side_effects=True, vmem_limit_bytes=62 * 1024 * 1024
         ),
-    )(fields, adjoints, couple, tmatrices, neighbours, classes.reshape(1, width))
+    )(fields, adjoints, couple, tmatrices, neighbours.T, classes.reshape(1, width))
 
 
 def solution(mesh):

time: 64.1 us -> 45 us (0.70)
  Pallas kernels: 55.9 us -> 41.3 us
  local copies, waits for them, and re-layouts: 7.17 us -> 2.65 us
    pallas_call x1, Pallas kernels: 55.9 us -> 41.3 us  [local(): pl.pallas_call(kernel, out_shape=(jax.ShapeDtypeStruct((rows, width), BF1...]
    unnamed x13 -> x2, local copies, waits for them, and re-layouts: 7.17 us -> 2.65 us
where the time goes in v2:
time: 45 us; the launch traced here: 44.6 us
  Pallas kernels  41.3 us (92%)
  local copies, waits for them, and re-layouts  2.65 us (6%)
  between operations  0.64 us (1%)
    pallas_call x1, Pallas kernels, local(): pl.pallas_call(kernel, out_shape=(jax.ShapeDtypeStruct((rows, width), BF1...  41.3 us
    unnamed x2, local copies, waits for them, and re-layouts  2.65 us

profile of v2, /device:TPU:1, one launch (start us, length us, event | category | flops | bytes accessed | tf_op | source)
XLA Modules:
  0.0 44.6 jit_solution(6006674318645241034)
XLA Ops:
  0.6 41.3 %shard_map.77 = (bf16[16,512]{1,0:T(8,128)(2,1)}, bf16[16,512]{1,0:T(8,128)(2,1)}) custom-call(bf16[16,512]{1,0:T(8,128)(2,1)} %fields_h.1, bf16[16,512]{1,0:T(8,128)(2,1)} %adj_h.1, bf16[30,256,256]{2,1,0:T(8,128)(2,1)} %couple_h.1, bf16[4,16,256]{2,1,0:T(8,128)(2,1)} %tmat_h.1, s32[30,512]{1,0:T(8,128)} %bitcast.2, s32[1,512]{1,0:T(1,128)} %bitcast.3), custom_call_target="tpu_custom_call" | custom-call | tf_op jit(solution)/shard_map/pallas_call | solution.py:232
  41.9 1.3 %copy.10 = bf16[16,512]{1,0:T(8,128)(2,1)} copy(bf16[16,512]{1,0:T(8,128)(2,1)} %get-tuple-element.4) | data formatting | bytes 32768
  43.2 1.3 %copy.11 = bf16[16,512]{1,0:T(8,128)(2,1)} copy(bf16[16,512]{1,0:T(8,128)(2,1)} %get-tuple-element.5) | data formatting | bytes 32768

commit v3 on v2

v3 whole, which is shorter than its diff:
```python
import jax
import jax.numpy as jnp
from jax import lax
from jax.experimental import pallas as pl
from jax.experimental.pallas import tpu as pltpu
from jax.sharding import PartitionSpec as P

SLOTS = 30
HW = 15
LANE = 128
MESH = pl.DeviceIdType.MESH
F32 = jnp.float32
BF16 = jnp.bfloat16


def dot(a, b, lhs=1, rhs=0):
    return lax.dot_general(a, b, (((lhs,), (rhs,)), ((), ())), preferred_element_type=F32)


def kernel(
    fields_h, adj_h, couple_h, tmat_h, nbr_h, cls_h, fwd_ref, adjo_ref,
    fields, adj, nbr, cls, rows_w, slab, cols_w, mask, t_all, tt_src, by_x, by_z, tt_all,
    edge_f, edge_a, edge_c, f_all, a_all, clsh, expanded, coup_all, s_all,
    load_sem, t_send, t_recv, tm_send, tm_recv, u_send, u_recv, um_send, um_recv,
    x_send, x_recv, z_send, z_recv, e_send, e_recv,
    f_send, f_recv, a_send, a_recv, c_send, c_recv, s_send, s_recv, z_known,
):
    rows, width = fields.shape
    wide = a_all.shape[1]
    t, c = lax.axis_index("tiles"), lax.axis_index("coef")
    x, z = c // 4, lax.rem(c, 4)
    mate = t + 1 - 2 * lax.rem(t, 2)

    def tile_at(step):
        return lax.rem(t + step, 16)

    def peer(dx, dz):
        return lax.rem(x + dx, 4) * 4 + lax.rem(z + dz, 4)

    def span(index, size):
        return pl.ds(pl.multiple_of(index * size, size), size)

    own = span(c, rows)
    lanes = span(c // 8, LANE)

    loads = [
        pltpu.make_async_copy(tmat_h, t_all.at[span(t, 4)], load_sem.at[0]),
        pltpu.make_async_copy(adj_h, adj, load_sem.at[1]),
        pltpu.make_async_copy(fields_h, fields, load_sem.at[2]),
        pltpu.make_async_copy(cls_h, cls, load_sem.at[3]),
        pltpu.make_async_copy(nbr_h, nbr, load_sem.at[4]),
        pltpu.make_async_copy(couple_h.at[:, :, lanes], slab, load_sem.at[5]),
        pltpu.make_async_copy(couple_h.at[:, own, :], rows_w, load_sem.at[6]),
    ]
    for load in loads:
        load.start()

    barrier = pltpu.get_barrier_semaphore()
    near_tiles, near_coef = (1, 15, 2, 4, 6, 8, 10, 12, 14), ((1, 0), (2, 0), (3, 0), (0, 1), (0, 3))
    for step in near_tiles:
        pl.semaphore_signal(barrier, inc=1, device_id=(tile_at(step), c), device_id_type=MESH)
    for dx, dz in near_coef:
        pl.semaphore_signal(barrier, inc=1, device_id=(t, peer(dx, dz)), device_id_type=MESH)
    for load in loads[:4]:
        load.wait()
    flat = t_all[span(t, 4)].reshape(4 * rows, 256)
    tt_src[...] = jnp.concatenate([flat, flat], axis=0).T
    pl.semaphore_wait(barrier, len(near_tiles) + len(near_coef))
    pl.semaphore_signal(z_known, inc=1, device_id=(t, peer(0, 1)), device_id_type=MESH)

    def remote(src, dst, send, recv, tile, coef):
        copy = pltpu.make_async_remote_copy(
            src_ref=src, dst_ref=dst, send_sem=send, recv_sem=recv,
            device_id=(tile, coef), device_id_type=MESH,
        )
        copy.start()
        return copy

    x_copies = [
        remote(tt_src.at[span(lax.rem(x + dx, 4), 64)], by_x.at[x], x_send.at[dx], x_recv.at[dx], t, peer(dx, 0))
        for dx in (2, 1, 3)
    ]
    edges = []
    for k, (src, dst) in enumerate(((adj, edge_a), (fields, edge_f), (cls, edge_c))):
        for side, (start, step) in enumerate(((0, 15), (width - LANE, 1))):
            slot = 2 * k + side
            edges.append(
                remote(src.at[:, pl.ds(start, LANE)], dst.at[side], e_send.at[slot], e_recv.at[slot], tile_at(step), c)
            )

    class Spread:
        def __init__(self, buf, size, send, recv, mate_send, mate_recv):
            self.buf, self.size = buf, size
            self.mate_send, self.mate_recv = mate_send, mate_recv
            mine = self.shard(t)
            self.copies = {s: remote(mine, mine, send.at[s], recv.at[s], tile_at(2 * s), c) for s in (4, 3, 5, 2, 6, 1, 7)}
            self.passed = [remote(mine, mine, mate_send.at[0], mate_recv.at[0], mate, c)]

        def shard(self, tile):
            return self.buf.at[span(tile, self.size)]

        def pass_on(self):
            for s in (1, 7, 2, 6, 3, 5, 4):
                self.copies[s].wait_recv()
                came = self.shard(tile_at(16 - 2 * s))
                self.passed.append(remote(came, came, self.mate_send.at[s], self.mate_recv.at[s], mate, c))

        def finish(self):
            for copy in self.passed:
                copy.wait_recv()

        def drain(self):
            for copy in list(self.copies.values()) + self.passed:
                copy.wait_send()

    class Gather:
        def __init__(self, buf, send, recv):
            self.copies = {}
            self.buf, self.send, self.recv = buf, send, recv

        def start(self, source, dx, dz, slot):
            block = self.buf.at[span(source, rows)]
            self.copies[slot] = remote(block, block, self.send.at[slot], self.recv.at[slot], t, peer(dx, dz))

        def begin(self):
            for dz in (2, 1, 3):
                self.start(c, 0, dz, dz)
            for dx in (2, 1, 3):
                self.start(c, dx, 0, 4 * dx)

        def relay(self):
            for dz in (1, 3, 2):
                self.copies[dz].wait_recv()
                for dx in (2, 1, 3):
                    self.start(peer(0, 4 - dz), dx, 0, 4 * dx + dz)

        def finish(self):
            for dz in (0, 1, 3, 2):
                for dx in (1, 3, 2):
                    self.copies[4 * dx + dz].wait_recv()

        def drain(self):
            for copy in self.copies.values():
                copy.wait_send()

    gather_f = Gather(f_all, f_send, f_recv)
    gather_a = Gather(a_all, a_send, a_recv)
    gather_c = Gather(coup_all, c_send, c_recv)
    gather_s = Gather(s_all, s_send, s_recv)

    t_rows = Spread(t_all, 4, t_send, t_recv, tm_send, tm_recv)

    by_x[x] = tt_src[span(x, 64)]
    a_all[own, :width] = adj[...]
    f_all[own, :width] = fields[...]
    clsh[:, :width] = cls[...]
    for copy in x_copies:
        copy.wait_recv()
    pl.semaphore_wait(z_known, 1)
    z_copies = [
        remote(by_x.at[:, span(lax.rem(z + dz, 4), rows), :], by_z.at[z], z_send.at[dz], z_recv.at[dz], t, peer(0, dz))
        for dz in (2, 1, 3)
    ]
    by_z[z] = by_x[:, span(z, rows), :]

    for edge in edges:
        edge.wait_recv()
    low = lax.broadcasted_iota(jnp.int32, (rows, LANE), 1) < LANE // 2
    low_row = lax.broadcasted_iota(jnp.int32, (1, LANE), 1) < LANE // 2
    a_all[own, width:] = jnp.where(low, edge_a[0], edge_a[1])
    f_all[own, width:] = jnp.where(low, edge_f[0], edge_f[1])
    clsh[:, width:] = jnp.where(low_row, edge_c[0], edge_c[1])
    gather_a.begin()
    gather_f.begin()

    loads[4].wait()
    mask[...] = (nbr[...] >= 0).astype(F32)
    loads[5].wait()
    loads[6].wait()
    pick = (
        lax.broadcasted_iota(jnp.int32, (rows, LANE), 1)
        == lax.broadcasted_iota(jnp.int32, (rows, LANE), 0) + lax.rem(c, 8) * rows
    ).astype(F32).astype(BF16)
    for m in range(SLOTS):
        cols_w[m] = dot(pick, slab[SLOTS - 1 - m], 1, 1).astype(BF16)

    t_rows.pass_on()
    for copy in z_copies:
        copy.wait_recv()
    for source_z in range(4):
        for half in range(2):
            block = jnp.where(low, by_z[source_z, 2 * half], by_z[source_z, 2 * half + 1])
            tt_all[span(t, rows), pl.ds((2 * source_z + half) * LANE, LANE)] = block
    t_cols = Spread(tt_all, rows, u_send, u_recv, um_send, um_recv)

    gather_a.relay()
    gather_f.relay()
    gather_a.finish()
    within = jnp.broadcast_to(jnp.bitwise_and(clsh[...], 3), (rows, wide))
    for source_z in range(4):
        for source_x in range(4):
            source = 4 * source_x + source_z
            values = a_all[source * rows : (source + 1) * rows].astype(F32)
            for k in range(4):
                at = ((4 * source_z + source_x) * 4 + k) * rows
                expanded[at : at + rows, :] = jnp.where(within == k, values, 0.0).astype(BF16)

    def coupling(weights, source):
        product = dot(weights, source)
        total = jnp.zeros((rows, width), F32)
        for m in range(SLOTS):
            shift = m - HW + (1 if m >= HW else 0)
            rolled = pltpu.roll(product[m * rows : (m + 1) * rows], (-shift) % wide, 1)
            total += rolled[:, :width] * mask[m : m + 1, :]
        return total

    gather_f.finish()
    coup_all[own, :] = coupling(rows_w[...].reshape(SLOTS * rows, 256), f_all[...]).astype(BF16)
    gather_c.begin()

    t_cols.pass_on()
    t_cols.finish()
    product = dot(tt_all[...], expanded[...])
    group = jnp.broadcast_to(lax.shift_right_arithmetic(clsh[...], jnp.full((1, wide), 2, jnp.int32)), (rows, wide))
    scattered = jnp.zeros((rows, wide), F32)
    for k in range(16):
        scattered += jnp.where(group == k, product[k * rows : (k + 1) * rows], 0.0)
    s_all[own, :] = scattered.astype(BF16)
    gather_s.begin()
    gather_c.relay()
    gather_s.relay()

    t_rows.finish()
    gather_c.finish()
    cls_own = jnp.broadcast_to(cls[...], (rows, width))
    applied = jnp.zeros((rows, width), F32)
    for b in range(4):
        product = dot(t_all[16 * b : 16 * b + 16].reshape(16 * rows, 256), coup_all[...])
        for k in range(16):
            applied += jnp.where(cls_own == 16 * b + k, product[k * rows : (k + 1) * rows], 0.0)
    fwd_ref[...] = (fields[...].astype(F32) - applied).astype(BF16)

    gather_s.finish()
    returned = coupling(cols_w[...].reshape(SLOTS * rows, 256), s_all[...])
    adjo_ref[...] = (adj[...].astype(F32) - returned).astype(BF16)

    for copy in x_copies + z_copies + edges:
        copy.wait_send()
    for group_copies in (t_rows, t_cols, gather_f, gather_a, gather_c, gather_s):
        group_copies.drain()


def hand_over(fwd_ref, adj_ref, fwd_out, adj_out, sem):
    copies = [
        pltpu.make_async_copy(fwd_ref, fwd_out, sem.at[0]),
        pltpu.make_async_copy(adj_ref, adj_out, sem.at[1]),
    ]
    for copy in copies:
        copy.start()
    for copy in copies:
        copy.wait()


def local(fields, adjoints, couple, tmatrices, neighbours, classes):
    rows, width = fields.shape
    wide = width + LANE
    kr = couple.shape[1]
    dma = pltpu.SemaphoreType.DMA
    anywhere = pl.BlockSpec(memory_space=pl.ANY)
    vmem = pl.BlockSpec(memory_space=pltpu.VMEM)
    outputs = (jax.ShapeDtypeStruct((rows, width), BF16),) * 2
    operands = (fields, adjoints, couple, tmatrices, neighbours.T, classes.reshape(1, width))
    results = pl.pallas_call(
        kernel,
        out_shape=outputs,
        in_specs=[anywhere] * 6,
        out_specs=(vmem, vmem),
        scratch_shapes=[
            pltpu.VMEM((rows, width), BF16),
            pltpu.VMEM((rows, width), BF16),
            pltpu.VMEM((SLOTS, width), jnp.int32),
            pltpu.VMEM((1, width), jnp.int32),
            pltpu.VMEM((SLOTS, rows, kr), BF16),
            pltpu.VMEM((SLOTS, kr, LANE), BF16),
            pltpu.VMEM((SLOTS, rows, kr), BF16),
            pltpu.VMEM((SLOTS, width), F32),
            pltpu.VMEM((64, rows, kr), BF16),
            pltpu.VMEM((kr, LANE), BF16),
            pltpu.VMEM((4, 64, LANE), BF16),
            pltpu.VMEM((4, 4, rows, LANE), BF16),
            pltpu.VMEM((kr, 1024), BF16),
            pltpu.VMEM((2, rows, LANE), BF16),
            pltpu.VMEM((2, rows, LANE), BF16),
            pltpu.VMEM((2, 1, LANE), jnp.int32),
            pltpu.VMEM((kr, wide), BF16),
            pltpu.VMEM((kr, wide), BF16),
            pltpu.VMEM((1, wide), jnp.int32),
            pltpu.VMEM((1024, wide), BF16),
            pltpu.VMEM((kr, width), BF16),
            pltpu.VMEM((kr, wide), BF16),
            dma((7,)),
        ]
        + [dma((8,))] * 8
        + [dma((4,))] * 4
        + [dma((6,))] * 2
        + [dma((16,))] * 8
        + [pltpu.SemaphoreType.REGULAR],
        compiler_params=pltpu.CompilerParams(
            collective_id=0, has_side_effects=True, vmem_limit_bytes=40 * 1024 * 1024
        ),
    )(*[pltpu.with_memory_space_constraint(v, pltpu.HBM) for v in operands])
    return pl.pallas_call(
        hand_over,
        out_shape=outputs,
        in_specs=[vmem, vmem],
        out_specs=(anywhere, anywhere),
        scratch_shapes=[dma((2,))],
        compiler_params=pltpu.CompilerParams(vmem_limit_bytes=1024 * 1024),
    )(*results)


def solution(mesh):
    placed = (
        P("coef", "tiles"),
        P("coef", "tiles"),
        P(),
        P("tiles", "coef", None),
        P("tiles", None),
        P("tiles"),
    )
    return jax.shard_map(
        local,
        mesh=mesh,
        in_specs=placed,
        out_specs=(P("coef", "tiles"), P("coef", "tiles")),
        check_vma=False,
    )
```

time: 45 us -> 41 us (0.911)
  local copies, waits for them, and re-layouts: 2.65 us -> 0 us
  Pallas kernels: 41.3 us -> 40.3 us
    unnamed x2 -> x0, local copies, waits for them, and re-layouts: 2.65 us -> none
    pallas_call x1 -> x2, Pallas kernels: 41.3 us -> 40.3 us  [the longest x1 39.6 us: local(): pl.pallas_call(kernel, out_shape=outputs, in_specs=[anywhere] * 6, out_sp...]
where the time goes in v3:
time: 41 us; the launch traced here: 40.9 us
  Pallas kernels  40.3 us (98%)
  between operations  0.64 us (2%)
    pallas_call x1, Pallas kernels, local(): pl.pallas_call(kernel, out_shape=outputs, in_specs=[anywhere] * 6, out_sp...  39.6 us

profile of v3, /device:TPU:1, one launch (start us, length us, event | category | flops | bytes accessed | tf_op | source)
XLA Modules:
  0.0 40.9 jit_solution(12346488810483447073)
XLA Ops:
  0.6 39.6 %shard_map.77 = (bf16[16,512]{1,0:T(8,128)(2,1)S(1)}, bf16[16,512]{1,0:T(8,128)(2,1)S(1)}) custom-call(bf16[16,512]{1,0:T(8,128)(2,1)} %fields_h.1, bf16[16,512]{1,0:T(8,128)(2,1)} %adj_h.1, bf16[30,256,256]{2,1,0:T(8,128)(2,1)} %couple_h.1, bf16[4,16,256]{2,1,0:T(8,128)(2,1)} %tmat_h.1, s32[30,512]{1,0:T(8,128)} %bitcast.2, s32[1,512]{1,0:T(1,128)} %bitcast.3), custom_call_target="tpu_custom_call" | custom-call | tf_op jit(solution)/shard_map/pallas_call | solution.py:273
  40.3 0.6 %shard_map.78 = (bf16[16,512]{1,0:T(8,128)(2,1)}, bf16[16,512]{1,0:T(8,128)(2,1)}) custom-call(bf16[16,512]{1,0:T(8,128)(2,1)S(1)} %get-tuple-element.4.fwd_ref, bf16[16,512]{1,0:T(8,128)(2,1)S(1)} %get-tuple-element.5.adj_ref), custom_call_target="tpu_custom_call" | custom-call | tf_op jit(solution)/shard_map/pallas_call | solution.py:312

commit v4 on v3

--- a/solution.py
+++ b/solution.py
@@ -20,13 +20,13 @@
 def kernel(
     fields_h, adj_h, couple_h, tmat_h, nbr_h, cls_h, fwd_ref, adjo_ref,
     fields, adj, nbr, cls, rows_w, slab, cols_w, mask, t_all, tt_src, by_x, by_z, tt_all,
-    edge_f, edge_a, edge_c, f_all, a_all, clsh, expanded, coup_all, s_all,
+    edge_f, edge_a, edge_c, af_all, ends_all, clsh, expanded, coup_all, s_all,
     load_sem, t_send, t_recv, tm_send, tm_recv, u_send, u_recv, um_send, um_recv,
     x_send, x_recv, z_send, z_recv, e_send, e_recv,
-    f_send, f_recv, a_send, a_recv, c_send, c_recv, s_send, s_recv, z_known,
+    g_send, g_recv, h_send, h_recv, c_send, c_recv, s_send, s_recv, z_known,
 ):
     rows, width = fields.shape
-    wide = a_all.shape[1]
+    wide = clsh.shape[1]
     t, c = lax.axis_index("tiles"), lax.axis_index("coef")
     x, z = c // 4, lax.rem(c, 4)
     mate = t + 1 - 2 * lax.rem(t, 2)
@@ -65,6 +65,8 @@
         load.wait()
     flat = t_all[span(t, 4)].reshape(4 * rows, 256)
     tt_src[...] = jnp.concatenate([flat, flat], axis=0).T
+    af_all[own, :width] = adj[...]
+    af_all[own, width:] = fields[...]
     pl.semaphore_wait(barrier, len(near_tiles) + len(near_coef))
     pl.semaphore_signal(z_known, inc=1, device_id=(t, peer(0, 1)), device_id_type=MESH)
 
@@ -75,6 +77,72 @@
         )
         copy.start()
         return copy
+
+    class Spread:
+        def __init__(self, shard, first, send, recv, mate_send, mate_recv):
+            self.shard, self.first = shard, first
+            self.mate_send, self.mate_recv = mate_send, mate_recv
+            mine = shard(t)
+            self.copies = {
+                s: remote(mine, mine, send.at[first + s], recv.at[first + s], tile_at(2 * s), c)
+                for s in (4, 3, 5, 2, 6, 1, 7)
+            }
+            self.passed = [remote(mine, mine, mate_send.at[first], mate_recv.at[first], mate, c)]
+
+        def pass_on(self):
+            for s in (1, 7, 2, 6, 3, 5, 4):
+                self.copies[s].wait_recv()
+                came, slot = self.shard(tile_at(16 - 2 * s)), self.first + s
+                self.passed.append(remote(came, came, self.mate_send.at[slot], self.mate_recv.at[slot], mate, c))
+
+        def finish(self):
+            for copy in self.passed:
+                copy.wait_recv()
+
+        def drain(self):
+            for copy in list(self.copies.values()) + self.passed:
+                copy.wait_send()
+
+    class Gather:
+        def __init__(self, buf, send, recv):
+            self.copies = {}
+            self.buf, self.send, self.recv = buf, send, recv
+
+        def start(self, source, dx, dz, slot):
+            block = self.buf.at[span(source, rows)]
+            self.copies[slot] = remote(block, block, self.send.at[slot], self.recv.at[slot], t, peer(dx, dz))
+
+        def along_z(self, *steps):
+            for dz in steps:
+                self.start(c, 0, dz, dz)
+
+        def along_x(self):
+            for dx in (2, 1, 3):
+                self.start(c, dx, 0, 4 * dx)
+
+        def begin(self):
+            self.along_z(2, 1, 3)
+            self.along_x()
+
+        def relay(self, *steps):
+            for dz in steps or (1, 3, 2):
+                self.copies[dz].wait_recv()
+                for dx in (2, 1, 3):
+                    self.start(peer(0, 4 - dz), dx, 0, 4 * dx + dz)
+
+        def finish(self):
+            for dz in (0, 1, 3, 2):
+                for dx in (1, 3, 2):
+                    self.copies[4 * dx + dz].wait_recv()
+
+        def drain(self):
+            for copy in self.copies.values():
+                copy.wait_send()
+
+    gather = Gather(af_all, g_send, g_recv)
+    gather_ends = Gather(ends_all, h_send, h_recv)
+    gather_c = Gather(coup_all, c_send, c_recv)
+    gather_s = Gather(s_all, s_send, s_recv)
 
     x_copies = [
         remote(tt_src.at[span(lax.rem(x + dx, 4), 64)], by_x.at[x], x_send.at[dx], x_recv.at[dx], t, peer(dx, 0))
@@ -88,90 +156,43 @@
                 remote(src.at[:, pl.ds(start, LANE)], dst.at[side], e_send.at[slot], e_recv.at[slot], tile_at(step), c)
             )
 
-    class Spread:
-        def __init__(self, buf, size, send, recv, mate_send, mate_recv):
-            self.buf, self.size = buf, size
-            self.mate_send, self.mate_recv = mate_send, mate_recv
-            mine = self.shard(t)
-            self.copies = {s: remote(mine, mine, send.at[s], recv.at[s], tile_at(2 * s), c) for s in (4, 3, 5, 2, 6, 1, 7)}
-            self.passed = [remote(mine, mine, mate_send.at[0], mate_recv.at[0], mate, c)]
-
-        def shard(self, tile):
-            return self.buf.at[span(tile, self.size)]
-
-        def pass_on(self):
-            for s in (1, 7, 2, 6, 3, 5, 4):
-                self.copies[s].wait_recv()
-                came = self.shard(tile_at(16 - 2 * s))
-                self.passed.append(remote(came, came, self.mate_send.at[s], self.mate_recv.at[s], mate, c))
-
-        def finish(self):
-            for copy in self.passed:
-                copy.wait_recv()
-
-        def drain(self):
-            for copy in list(self.copies.values()) + self.passed:
-                copy.wait_send()
-
-    class Gather:
-        def __init__(self, buf, send, recv):
-            self.copies = {}
-            self.buf, self.send, self.recv = buf, send, recv
-
-        def start(self, source, dx, dz, slot):
-            block = self.buf.at[span(source, rows)]
-            self.copies[slot] = remote(block, block, self.send.at[slot], self.recv.at[slot], t, peer(dx, dz))
-
-        def begin(self):
-            for dz in (2, 1, 3):
-                self.start(c, 0, dz, dz)
-            for dx in (2, 1, 3):
-                self.start(c, dx, 0, 4 * dx)
-
-        def relay(self):
-            for dz in (1, 3, 2):
-                self.copies[dz].wait_recv()
-                for dx in (2, 1, 3):
-                    self.start(peer(0, 4 - dz), dx, 0, 4 * dx + dz)
-
-        def finish(self):
-            for dz in (0, 1, 3, 2):
-                for dx in (1, 3, 2):
-                    self.copies[4 * dx + dz].wait_recv()
-
-        def drain(self):
-            for copy in self.copies.values():
-                copy.wait_send()
-
-    gather_f = Gather(f_all, f_send, f_recv)
-    gather_a = Gather(a_all, a_send, a_recv)
-    gather_c = Gather(coup_all, c_send, c_recv)
-    gather_s = Gather(s_all, s_send, s_recv)
-
-    t_rows = Spread(t_all, 4, t_send, t_recv, tm_send, tm_recv)
-
     by_x[x] = tt_src[span(x, 64)]
-    a_all[own, :width] = adj[...]
-    f_all[own, :width] = fields[...]
     clsh[:, :width] = cls[...]
+    gather.along_z(1, 3)
+    gather.along_x()
     for copy in x_copies:
         copy.wait_recv()
     pl.semaphore_wait(z_known, 1)
-    z_copies = [
-        remote(by_x.at[:, span(lax.rem(z + dz, 4), rows), :], by_z.at[z], z_send.at[dz], z_recv.at[dz], t, peer(0, dz))
+    z_copies = {
+        dz: remote(by_x.at[:, span(lax.rem(z + dz, 4), rows), :], by_z.at[z], z_send.at[dz], z_recv.at[dz], t, peer(0, dz))
         for dz in (2, 1, 3)
-    ]
+    }
+    gather.along_z(2)
     by_z[z] = by_x[:, span(z, rows), :]
+    low = lax.broadcasted_iota(jnp.int32, (rows, LANE), 1) < LANE // 2
+    t_cols = {}
+
+    def spread_quarter(dz):
+        if dz:
+            z_copies[dz].wait_recv()
+        source_z = lax.rem(z + 4 - dz, 4)
+        for half in range(2):
+            block = jnp.where(low, by_z[source_z, 2 * half], by_z[source_z, 2 * half + 1])
+            tt_all[source_z, span(t, rows), half * LANE : (half + 1) * LANE] = block
+        t_cols[dz] = Spread(
+            lambda tile: tt_all.at[source_z, span(tile, rows)], 8 * dz, u_send, u_recv, um_send, um_recv
+        )
+
+    spread_quarter(0)
 
     for edge in edges:
         edge.wait_recv()
-    low = lax.broadcasted_iota(jnp.int32, (rows, LANE), 1) < LANE // 2
     low_row = lax.broadcasted_iota(jnp.int32, (1, LANE), 1) < LANE // 2
-    a_all[own, width:] = jnp.where(low, edge_a[0], edge_a[1])
-    f_all[own, width:] = jnp.where(low, edge_f[0], edge_f[1])
+    ends_all[own, :LANE] = jnp.where(low, edge_a[0], edge_a[1])
+    ends_all[own, LANE:] = jnp.where(low, edge_f[0], edge_f[1])
     clsh[:, width:] = jnp.where(low_row, edge_c[0], edge_c[1])
-    gather_a.begin()
-    gather_f.begin()
+    gather_ends.begin()
+    gather.relay(1, 3)
 
     loads[4].wait()
     mask[...] = (nbr[...] >= 0).astype(F32)
@@ -184,29 +205,15 @@
     for m in range(SLOTS):
         cols_w[m] = dot(pick, slab[SLOTS - 1 - m], 1, 1).astype(BF16)
 
-    t_rows.pass_on()
-    for copy in z_copies:
-        copy.wait_recv()
-    for source_z in range(4):
-        for half in range(2):
-            block = jnp.where(low, by_z[source_z, 2 * half], by_z[source_z, 2 * half + 1])
-            tt_all[span(t, rows), pl.ds((2 * source_z + half) * LANE, LANE)] = block
-    t_cols = Spread(tt_all, rows, u_send, u_recv, um_send, um_recv)
-
-    gather_a.relay()
-    gather_f.relay()
-    gather_a.finish()
-    within = jnp.broadcast_to(jnp.bitwise_and(clsh[...], 3), (rows, wide))
-    for source_z in range(4):
-        for source_x in range(4):
-            source = 4 * source_x + source_z
-            values = a_all[source * rows : (source + 1) * rows].astype(F32)
-            for k in range(4):
-                at = ((4 * source_z + source_x) * 4 + k) * rows
-                expanded[at : at + rows, :] = jnp.where(within == k, values, 0.0).astype(BF16)
-
-    def coupling(weights, source):
-        product = dot(weights, source)
+    spread_quarter(1)
+    spread_quarter(3)
+    spread_quarter(2)
+    t_rows = Spread(lambda tile: t_all.at[span(tile, 4)], 0, t_send, t_recv, tm_send, tm_recv)
+    gather.relay(2)
+    gather_ends.relay()
+
+    def coupling(weights, inner, ends):
+        product = jnp.concatenate([dot(weights, inner), dot(weights, ends)], axis=1)
         total = jnp.zeros((rows, width), F32)
         for m in range(SLOTS):
             shift = m - HW + (1 if m >= HW else 0)
@@ -214,19 +221,44 @@
             total += rolled[:, :width] * mask[m : m + 1, :]
         return total
 
-    gather_f.finish()
-    coup_all[own, :] = coupling(rows_w[...].reshape(SLOTS * rows, 256), f_all[...]).astype(BF16)
+    for dz in (0, 1, 3):
+        t_cols[dz].pass_on()
+    gather.finish()
+    within = jnp.broadcast_to(jnp.bitwise_and(clsh[...], 3), (rows, wide))
+    for source_z in range(4):
+        for source_x in range(4):
+            source = 4 * source_x + source_z
+            block = slice(source * rows, (source + 1) * rows)
+            values = af_all[block, :width].astype(F32)
+            for k in range(4):
+                at = ((4 * source_z + source_x) * 4 + k) * rows
+                expanded[at : at + rows, :width] = jnp.where(within[:, :width] == k, values, 0.0).astype(BF16)
+    t_cols[2].pass_on()
+    gather_ends.finish()
+    own_rows = rows_w[...].reshape(SLOTS * rows, 256)
+    coup_all[own, :] = coupling(own_rows, af_all[:, width:], ends_all[:, LANE:]).astype(BF16)
     gather_c.begin()
 
-    t_cols.pass_on()
-    t_cols.finish()
-    product = dot(tt_all[...], expanded[...])
+    for source_z in range(4):
+        for source_x in range(4):
+            source = 4 * source_x + source_z
+            block = slice(source * rows, (source + 1) * rows)
+            values = ends_all[block, :LANE].astype(F32)
+            for k in range(4):
+                at = ((4 * source_z + source_x) * 4 + k) * rows
+                expanded[at : at + rows, width:] = jnp.where(within[:, width:] == k, values, 0.0).astype(BF16)
+    product = jnp.zeros((256, wide), F32)
+    for dz in (0, 1, 3, 2):
+        t_cols[dz].finish()
+        quarter = lax.rem(z + 4 - dz, 4)
+        product += dot(tt_all[quarter], expanded[span(quarter, 256)])
     group = jnp.broadcast_to(lax.shift_right_arithmetic(clsh[...], jnp.full((1, wide), 2, jnp.int32)), (rows, wide))
     scattered = jnp.zeros((rows, wide), F32)
     for k in range(16):
         scattered += jnp.where(group == k, product[k * rows : (k + 1) * rows], 0.0)
     s_all[own, :] = scattered.astype(BF16)
     gather_s.begin()
+    t_rows.pass_on()
     gather_c.relay()
     gather_s.relay()
 
@@ -241,12 +273,12 @@
     fwd_ref[...] = (fields[...].astype(F32) - applied).astype(BF16)
 
     gather_s.finish()
-    returned = coupling(cols_w[...].reshape(SLOTS * rows, 256), s_all[...])
+    returned = coupling(cols_w[...].reshape(SLOTS * rows, 256), s_all[:, :width], s_all[:, width:])
     adjo_ref[...] = (adj[...].astype(F32) - returned).astype(BF16)
 
-    for copy in x_copies + z_copies + edges:
+    for copy in x_copies + list(z_copies.values()) + edges:
         copy.wait_send()
-    for group_copies in (t_rows, t_cols, gather_f, gather_a, gather_c, gather_s):
+    for group_copies in (t_rows, *t_cols.values(), gather, gather_ends, gather_c, gather_s):
         group_copies.drain()
 
 
@@ -288,19 +320,20 @@
             pltpu.VMEM((kr, LANE), BF16),
             pltpu.VMEM((4, 64, LANE), BF16),
             pltpu.VMEM((4, 4, rows, LANE), BF16),
-            pltpu.VMEM((kr, 1024), BF16),
+            pltpu.VMEM((4, kr, 256), BF16),
             pltpu.VMEM((2, rows, LANE), BF16),
             pltpu.VMEM((2, rows, LANE), BF16),
             pltpu.VMEM((2, 1, LANE), jnp.int32),
-            pltpu.VMEM((kr, wide), BF16),
-            pltpu.VMEM((kr, wide), BF16),
+            pltpu.VMEM((kr, 2 * width), BF16),
+            pltpu.VMEM((kr, 2 * LANE), BF16),
             pltpu.VMEM((1, wide), jnp.int32),
             pltpu.VMEM((1024, wide), BF16),
             pltpu.VMEM((kr, width), BF16),
             pltpu.VMEM((kr, wide), BF16),
             dma((7,)),
         ]
-        + [dma((8,))] * 8
+        + [dma((8,))] * 4
+        + [dma((32,))] * 4
         + [dma((4,))] * 4
         + [dma((6,))] * 2
         + [dma((16,))] * 8

time: 41 us -> 38.7 us (0.944)
  the two profiles are of different devices: /device:TPU:1 before, /device:TPU:16 now
where the time goes in v4:
time: 38.7 us; the launch traced here: 38.6 us
  Pallas kernels  38 us (98%)
  between operations  0.64 us (2%)
    pallas_call x1, Pallas kernels, local(): pl.pallas_call(kernel, out_shape=outputs, in_specs=[anywhere] * 6, out_sp...  37.3 us

profile of v4, /device:TPU:16, one launch (start us, length us, event | category | flops | bytes accessed | tf_op | source)
XLA Modules:
  0.0 38.6 jit_solution(12883013782676996752)
XLA Ops:
  0.6 37.3 %shard_map.77 = (bf16[16,512]{1,0:T(8,128)(2,1)S(1)}, bf16[16,512]{1,0:T(8,128)(2,1)S(1)}) custom-call(bf16[16,512]{1,0:T(8,128)(2,1)} %fields_h.1, bf16[16,512]{1,0:T(8,128)(2,1)} %adj_h.1, bf16[30,256,256]{2,1,0:T(8,128)(2,1)} %couple_h.1, bf16[4,16,256]{2,1,0:T(8,128)(2,1)} %tmat_h.1, s32[30,512]{1,0:T(8,128)} %bitcast.2, s32[1,512]{1,0:T(1,128)} %bitcast.3), custom_call_target="tpu_custom_call" | custom-call | tf_op jit(solution)/shard_map/pallas_call | solution.py:305
  38.0 0.6 %shard_map.78 = (bf16[16,512]{1,0:T(8,128)(2,1)}, bf16[16,512]{1,0:T(8,128)(2,1)}) custom-call(bf16[16,512]{1,0:T(8,128)(2,1)S(1)} %get-tuple-element.4.fwd_ref, bf16[16,512]{1,0:T(8,128)(2,1)S(1)} %get-tuple-element.5.adj_ref), custom_call_target="tpu_custom_call" | custom-call | tf_op jit(solution)/shard_map/pallas_call | solution.py:345

commit v5 on v4

--- a/solution.py
+++ b/solution.py
@@ -224,6 +224,11 @@
     for dz in (0, 1, 3):
         t_cols[dz].pass_on()
     gather.finish()
+    t_cols[2].pass_on()
+    gather_ends.finish()
+    own_rows = rows_w[...].reshape(SLOTS * rows, 256)
+    coup_all[own, :] = coupling(own_rows, af_all[:, width:], ends_all[:, LANE:]).astype(BF16)
+    gather_c.begin()
     within = jnp.broadcast_to(jnp.bitwise_and(clsh[...], 3), (rows, wide))
     for source_z in range(4):
         for source_x in range(4):
@@ -233,11 +238,6 @@
             for k in range(4):
                 at = ((4 * source_z + source_x) * 4 + k) * rows
                 expanded[at : at + rows, :width] = jnp.where(within[:, :width] == k, values, 0.0).astype(BF16)
-    t_cols[2].pass_on()
-    gather_ends.finish()
-    own_rows = rows_w[...].reshape(SLOTS * rows, 256)
-    coup_all[own, :] = coupling(own_rows, af_all[:, width:], ends_all[:, LANE:]).astype(BF16)
-    gather_c.begin()
 
     for source_z in range(4):
         for source_x in range(4):
@@ -258,10 +258,10 @@
         scattered += jnp.where(group == k, product[k * rows : (k + 1) * rows], 0.0)
     s_all[own, :] = scattered.astype(BF16)
     gather_s.begin()
-    t_rows.pass_on()
     gather_c.relay()
     gather_s.relay()
 
+    t_rows.pass_on()
     t_rows.finish()
     gather_c.finish()
     cls_own = jnp.broadcast_to(cls[...], (rows, width))

time: 38.7 us -> 38.5 us (level)
  no operation moved by 1% of the time
where the time goes in v5:
time: 38.5 us; the launch traced here: 38.4 us
  Pallas kernels  37.8 us (98%)
  between operations  0.64 us (2%)
    pallas_call x1, Pallas kernels, local(): pl.pallas_call(kernel, out_shape=outputs, in_specs=[anywhere] * 6, out_sp...  37.1 us

profile of v5, /device:TPU:16, one launch (start us, length us, event | category | flops | bytes accessed | tf_op | source)
XLA Modules:
  0.0 38.4 jit_solution(9338417078211652847)
XLA Ops:
  0.6 37.1 %shard_map.77 = (bf16[16,512]{1,0:T(8,128)(2,1)S(1)}, bf16[16,512]{1,0:T(8,128)(2,1)S(1)}) custom-call(bf16[16,512]{1,0:T(8,128)(2,1)} %fields_h.1, bf16[16,512]{1,0:T(8,128)(2,1)} %adj_h.1, bf16[30,256,256]{2,1,0:T(8,128)(2,1)} %couple_h.1, bf16[4,16,256]{2,1,0:T(8,128)(2,1)} %tmat_h.1, s32[30,512]{1,0:T(8,128)} %bitcast.2, s32[1,512]{1,0:T(1,128)} %bitcast.3), custom_call_target="tpu_custom_call" | custom-call | tf_op jit(solution)/shard_map/pallas_call | solution.py:305
  37.8 0.6 %shard_map.78 = (bf16[16,512]{1,0:T(8,128)(2,1)}, bf16[16,512]{1,0:T(8,128)(2,1)}) custom-call(bf16[16,512]{1,0:T(8,128)(2,1)S(1)} %get-tuple-element.4.fwd_ref, bf16[16,512]{1,0:T(8,128)(2,1)S(1)} %get-tuple-element.5.adj_ref), custom_call_target="tpu_custom_call" | custom-call | tf_op jit(solution)/shard_map/pallas_call | solution.py:345

commit v6 on v5

--- a/solution.py
+++ b/solution.py
@@ -159,7 +159,6 @@
     by_x[x] = tt_src[span(x, 64)]
     clsh[:, :width] = cls[...]
     gather.along_z(1, 3)
-    gather.along_x()
     for copy in x_copies:
         copy.wait_recv()
     pl.semaphore_wait(z_known, 1)
@@ -168,6 +167,7 @@
         for dz in (2, 1, 3)
     }
     gather.along_z(2)
+    gather.along_x()
     by_z[z] = by_x[:, span(z, rows), :]
     low = lax.broadcasted_iota(jnp.int32, (rows, LANE), 1) < LANE // 2
     t_cols = {}

time: 38.5 us -> 38.5 us (level)
  the two profiles are of different devices: /device:TPU:16 before, /device:TPU:24 now
where the time goes in v6:
time: 38.5 us; the launch traced here: 38.4 us
  Pallas kernels  37.8 us (98%)
  between operations  0.64 us (2%)
    pallas_call x1, Pallas kernels, local(): pl.pallas_call(kernel, out_shape=outputs, in_specs=[anywhere] * 6, out_sp...  37.1 us

profile of v6, /device:TPU:24, one launch (start us, length us, event | category | flops | bytes accessed | tf_op | source)
XLA Modules:
  0.0 38.4 jit_solution(11907292850784787894)
XLA Ops:
  0.6 37.1 %shard_map.77 = (bf16[16,512]{1,0:T(8,128)(2,1)S(1)}, bf16[16,512]{1,0:T(8,128)(2,1)S(1)}) custom-call(bf16[16,512]{1,0:T(8,128)(2,1)} %fields_h.1, bf16[16,512]{1,0:T(8,128)(2,1)} %adj_h.1, bf16[30,256,256]{2,1,0:T(8,128)(2,1)} %couple_h.1, bf16[4,16,256]{2,1,0:T(8,128)(2,1)} %tmat_h.1, s32[30,512]{1,0:T(8,128)} %bitcast.2, s32[1,512]{1,0:T(1,128)} %bitcast.3), custom_call_target="tpu_custom_call" | custom-call | tf_op jit(solution)/shard_map/pallas_call | solution.py:305
  37.8 0.6 %shard_map.78 = (bf16[16,512]{1,0:T(8,128)(2,1)}, bf16[16,512]{1,0:T(8,128)(2,1)}) custom-call(bf16[16,512]{1,0:T(8,128)(2,1)S(1)} %get-tuple-element.4.fwd_ref, bf16[16,512]{1,0:T(8,128)(2,1)S(1)} %get-tuple-element.5.adj_ref), custom_call_target="tpu_custom_call" | custom-call | tf_op jit(solution)/shard_map/pallas_call | solution.py:345
